TPU v7x, 128 devices: a whole 4x4x4 slice. The times are simulated.
128 devices in a mesh: group: 16 (over y_hi, x, core), mp: 8 (over z, y_lo).
Axes of the slice: x: 4, y: 4 (y_hi: 2, y_lo: 2; y = y_hi * 2 + y_lo), z: 4, core: 2. Of those that a mesh axis runs over, the one named last changes fastest.
Arguments:
- hidden_in: bfloat16 [8192, 1024], P('group'), may hold values from -8 to 8
- request_ids: int32 [8192], P('group'), may hold values from 63 to 8191, as said below
- w_qkv: float32 [1024, 3072], P(('group', 'mp')), may hold values from -1 to 1
- w_out: float32 [1024, 1024], P(('group', 'mp')), may hold values from -0.1875 to 0.1875
- w_up: float32 [1024, 4096], P(('group', 'mp')), may hold values from -0.1875 to 0.1875
- w_down: float32 [1024, 4096], P(('group', 'mp')), may hold values from -0.09375 to 0.09375
- ln1_gain: float32 [1024], replicated, may hold values from 0.25 to 1.75
- ln1_shift: float32 [1024], replicated, may hold values from -3 to 3
- ln2_gain: float32 [1024], replicated, may hold values from 0.25 to 1.75
- ln2_shift: float32 [1024], replicated, may hold values from -3 to 3
Outputs:
- hidden_out: bfloat16 [8192, 1024], P(('group', 'mp'))
- keys_cache: bfloat16 [8192, 1024], P('group', 'mp')
- values_cache: bfloat16 [8192, 1024], P('group', 'mp')
Inputs may be any that keep to these rules, and one draw needn't show every extreme that they name: `request_ids`: each slot holds the index of the last slot of its request. In groups 2i and 2i+1 (of 512 slots each) one request of exactly 512 slots ends the first group and begins the second, at least 64 of its slots in each; every other request lies within one aligned block of 64 slots, one or two requests a block, and some blocks hold one request of exactly 64 slots.
All inputs are finite; a program needn't handle non-finite values.
Results may differ from a plain program's by a relative error of at most 0.011.
Values may be sent and summed in bfloat16 or wider, within the bound.
No kernel may reach another device: no remote copies, remote signals or barrier semaphores. Data moves between devices by JAX's collectives and lax.ppermute only.
A program may use at most 64 MiB of HBM per device.

v0:
```python
import jax
import jax.numpy as jnp
from jax import lax
from jax.sharding import PartitionSpec as P

HD = 64
SHORT = 64


def swapped(value, axis, distance):
    return lax.ppermute(value, axis, [(i, i ^ 1 << distance) for i in range(lax.axis_size(axis))])


def layer_norm(values_in, norm_gain, norm_shift):
    center = values_in - jnp.mean(values_in, axis=-1, keepdims=True)
    spread = jnp.mean(center * center, axis=-1, keepdims=True)
    return center * lax.rsqrt(spread + 1e-05) * norm_gain + norm_shift


def body(
    hidden_in, request_ids, w_qkv, w_out, w_up, w_down, ln1_gain, ln1_shift, ln2_gain, ln2_shift
):
    groups = lax.axis_size("group")
    shards = lax.axis_size("mp")
    model_width = hidden_in.shape[1]
    local_width = model_width // shards
    local_hidden = w_up.shape[1] // shards
    tok_rows = hidden_in.shape[0]
    part_rows = w_qkv.shape[0]
    pieces = (
        w_qkv.astype(jnp.bfloat16).reshape(part_rows, 3, shards, local_width),
        w_out.astype(jnp.bfloat16).reshape(part_rows, 1, shards, local_width),
        w_up.astype(jnp.bfloat16).reshape(part_rows, 1, shards, local_hidden),
        w_down.astype(jnp.bfloat16).reshape(part_rows, 1, shards, local_hidden),
    )
    gathered = (
        lax.all_gather(pieces[0], "group", axis=0, tiled=True),
        lax.all_gather(pieces[1], "group", axis=0, tiled=True),
        lax.all_gather(pieces[2], "group", axis=0, tiled=True),
        lax.all_gather(pieces[3], "group", axis=0, tiled=True),
    )
    exchanged = (
        lax.all_to_all(gathered[0], "mp", split_axis=2, concat_axis=0, tiled=True),
        lax.all_to_all(gathered[1], "mp", split_axis=2, concat_axis=0, tiled=True),
        lax.all_to_all(gathered[2], "mp", split_axis=2, concat_axis=0, tiled=True),
        lax.all_to_all(gathered[3], "mp", split_axis=2, concat_axis=0, tiled=True),
    )
    served = tuple(
        (
            jnp.transpose(
                weight_piece.reshape(shards, groups, part_rows, -1), (1, 0, 2, 3)
            ).reshape(model_width, -1)
            for weight_piece in exchanged
        )
    )
    qkv_local, out_local, up_local, down_local = served
    projected = jnp.dot(hidden_in, qkv_local, preferred_element_type=jnp.float32)
    queries = projected[:, :local_width].astype(jnp.bfloat16)
    key_rows = projected[:, local_width : 2 * local_width].astype(jnp.bfloat16)
    value_rows = projected[:, 2 * local_width :].astype(jnp.bfloat16)
    partner_keys, partner_values = swapped((key_rows, value_rows), "group", 0)
    group_index = lax.axis_index("group")
    parity = group_index % 2
    long_id = jnp.where(parity == 0, request_ids[-1], request_ids[0])
    own_long = request_ids == long_id
    local_heads = local_width // HD
    score_scale = HD ** (-0.5)
    block_total = tok_rows // SHORT
    short_q = queries.reshape(block_total, SHORT, local_heads, HD)
    short_k = key_rows.reshape(block_total, SHORT, local_heads, HD)
    short_v = value_rows.reshape(block_total, SHORT, local_heads, HD)
    short_ids = request_ids.reshape(block_total, SHORT)
    short_scores = (
        jnp.einsum("bqhd,bkhd->bhqk", short_q, short_k, preferred_element_type=jnp.float32)
        * score_scale
    )
    short_mask = short_ids[:, :, None] == short_ids[:, None, :]
    short_scores = jnp.where(short_mask[:, None], short_scores, -1e30)
    short_peak = jnp.max(short_scores, axis=-1, keepdims=True)
    short_weights = jnp.exp(short_scores - short_peak).astype(jnp.bfloat16)
    short_totals = jnp.sum(short_weights.astype(jnp.float32), axis=-1)
    short_mixed = jnp.einsum(
        "bhqk,bkhd->bqhd", short_weights, short_v, preferred_element_type=jnp.float32
    )
    short_out = (
        (short_mixed / jnp.transpose(short_totals, (0, 2, 1))[:, :, :, None])
        .astype(jnp.bfloat16)
        .reshape(tok_rows, local_width)
    )
    first_keys = jnp.where(parity == 0, key_rows, partner_keys)
    second_keys = jnp.where(parity == 0, partner_keys, key_rows)
    first_values = jnp.where(parity == 0, value_rows, partner_values)
    second_values = jnp.where(parity == 0, partner_values, value_rows)
    pair_base = (group_index - parity) * tok_rows
    span_start = long_id - tok_rows + 1 - pair_base
    long_keys = lax.dynamic_slice_in_dim(
        jnp.concatenate([first_keys, second_keys], 0), span_start, tok_rows, 0
    ).reshape(tok_rows, local_heads, HD)
    long_values = lax.dynamic_slice_in_dim(
        jnp.concatenate([first_values, second_values], 0), span_start, tok_rows, 0
    ).reshape(tok_rows, local_heads, HD)
    query_rows = min(512, tok_rows)
    query_blocks = tok_rows // query_rows

    def long_attend(block_queries):
        heads_view = block_queries.reshape(query_rows, local_heads, HD)
        scores = (
            jnp.einsum("qhd,khd->hqk", heads_view, long_keys, preferred_element_type=jnp.float32)
            * score_scale
        )
        row_peak = jnp.max(scores, axis=-1, keepdims=True)
        weights = jnp.exp(scores - row_peak).astype(jnp.bfloat16)
        totals = jnp.sum(weights.astype(jnp.float32), axis=-1)
        mixed_heads = jnp.einsum(
            "hqk,khd->qhd", weights, long_values, preferred_element_type=jnp.float32
        )
        return (
            (mixed_heads / jnp.transpose(totals)[:, :, None])
            .astype(jnp.bfloat16)
            .reshape(query_rows, local_width)
        )

    def skipped(block_queries):
        return jnp.zeros((query_rows, local_width), jnp.bfloat16)

    def long_block(query_block):
        block_queries, block_long = query_block
        return lax.cond(jnp.any(block_long), long_attend, skipped, block_queries)

    long_out = lax.map(
        long_block,
        (
            queries.reshape(query_blocks, query_rows, local_width),
            own_long.reshape(query_blocks, query_rows),
        ),
    ).reshape(tok_rows, local_width)
    attended = jnp.where(own_long[:, None], long_out, short_out)
    share_rows = tok_rows // shards
    row_start = lax.axis_index("mp") * share_rows

    def combine(term_fn, residual, norm_gain, norm_shift):
        summed = lax.psum(term_fn(0, tok_rows), "mp")
        whole_rows = layer_norm(
            residual.astype(jnp.float32) + summed, norm_gain, norm_shift
        ).astype(jnp.bfloat16)
        normed = lax.dynamic_slice_in_dim(whole_rows, row_start, share_rows, 0)
        return (normed, whole_rows)

    def attn_term(row_begin, row_count):
        return lax.dot_general(
            attended, out_local, (((1,), (1,)), ((), ())), preferred_element_type=jnp.float32
        )

    attn_share, attn_normed = combine(attn_term, hidden_in, ln1_gain, ln1_shift)
    activated = jax.nn.gelu(
        jnp.dot(attn_normed, up_local, preferred_element_type=jnp.float32), approximate=False
    ).astype(jnp.bfloat16)

    def feed_term(row_begin, row_count):
        return lax.dot_general(
            activated, down_local, (((1,), (1,)), ((), ())), preferred_element_type=jnp.float32
        )

    final_share, unused = combine(feed_term, attn_normed, ln2_gain, ln2_shift)
    return (final_share, key_rows, value_rows)


def solution(mesh):
    in_specs = (
        P("group", None),
        P("group"),
        P(("group", "mp"), None),
        P(("group", "mp"), None),
        P(("group", "mp"), None),
        P(("group", "mp"), None),
        P(),
        P(),
        P(),
        P(),
    )
    out_specs = (P(("group", "mp"), None), P("group", "mp"), P("group", "mp"))
    return jax.shard_map(body, mesh=mesh, in_specs=in_specs, out_specs=out_specs, check_vma=False)
```

profile of v0, /device:TPU:1, one launch (start us, length us, event | category | flops | bytes accessed | tf_op | source)
XLA Modules:
  0.0 345.1 jit_solution(3405241490203082044)
XLA Ops:
  8.0 1.5 convert_element_type.73
  9.6 0.8 convert_bitcast_fusion.1
  10.4 27.8 %all_gather.13 = bf16[128,1,8,128]{3,0,1,2:T(8,128)(2,1)} all-gather(bf16[8,1,8,128]{3,0,1,2:T(8,128)(2,1)S(1)} %convert_bitcast_fusion.1), channel_id=1, replica_groups=mesh['group'=16,'mp'=8] {'group'}, dimensions={0}, use_global_device_ids=true | all-gather | bytes 278528 | tf_op jit(solution)/shard_map/all_gather | solution.py:38
  38.1 5.1 %all-to-all-start.1 = ((bf16[128,1,8,128]{3,0,1,2:T(8,128)(2,1)}), bf16[128,1,8,128]{3,0,1,2:T(8,128)(2,1)S(1)}, u32[]{:S(2)}, u32[]{:S(2)}) async-start(bf16[128,1,8,128]{3,0,1,2:T(8,128)(2,1)} %all_gather.13), calls=%async_computation.1 | async-start | bytes 524288 | tf_op jit(solution)/shard_map/all_to_all | solution.py:44
  43.3 0.9 convert_bitcast_fusion
  44.2 22.1 %all_gather.12 = bf16[128,3,8,128]{3,2,1,0:T(8,128)(2,1)S(1)} all-gather(bf16[8,3,8,128]{3,2,1,0:T(8,128)(2,1)S(1)} %bitcast.100), channel_id=1, replica_groups=mesh['group'=16,'mp'=8] {'group'}, dimensions={0}, use_global_device_ids=true | all-gather | bytes 835584 | tf_op jit(solution)/shard_map/all_gather | solution.py:37
  66.3 1.1 copy.76
  67.4 5.8 %all-to-all-start = ((bf16[128,3,8,128]{3,0,1,2:T(8,128)(2,1)}), bf16[128,3,8,128]{3,0,1,2:T(8,128)(2,1)S(1)}, u32[]{:S(2)}, u32[]{:S(2)}) async-start(bf16[128,3,8,128]{3,0,1,2:T(8,128)(2,1)} %copy.76), calls=%async_computation | async-start | bytes 1572864 | tf_op jit(solution)/shard_map/all_to_all | solution.py:43
  73.2 0.6 convert_element_type.75
  74.1 0.6 fusion.98
  75.9 0.6 fusion.96
  77.4 8.3 %all-to-all-done = bf16[128,3,8,128]{3,0,1,2:T(8,128)(2,1)S(1)} async-done(((bf16[128,3,8,128]{3,0,1,2:T(8,128)(2,1)}), bf16[128,3,8,128]{3,0,1,2:T(8,128)(2,1)S(1)}, u32[]{:S(2)}, u32[]{:S(2)}) %all-to-all-start) | async-done | bytes 786464 | tf_op jit(solution)/shard_map/all_to_all | solution.py:43
  85.8 0.7 copy.77
  86.5 0.7 reshape.140
  87.3 0.4 copy-done.1
  87.7 0.7 convolution_convert_fusion
  88.5 1.4 collective-permute-start
  90.4 0.3 fusion.9
  90.7 0.1 convert_reduce_fusion.1
  90.8 0.6 copy-done.12
  91.4 1.5 fusion.10
  92.9 0.2 copy.86
  93.1 0.2 reshape.145
  93.5 2.0 conditional.1
  93.8 0.2 constant_dynamic-slice_fusion
  94.1 0.5 bitcast_reduce_fusion
  94.6 0.4 convert_reduce_fusion
  95.0 0.5 fusion.3
  95.5 1.8 fusion.61
  97.3 3.6 %all-to-all-start.2 = ((bf16[128,1,8,512]{3,0,1,2:T(8,128)(2,1)}), bf16[128,1,8,512]{3,0,1,2:T(8,128)(2,1)S(1)}, u32[]{:S(2)}, u32[]{:S(2)}) async-start(bf16[128,1,8,512]{3,0,1,2:T(8,128)(2,1)} %all-gather.3.cloned.1.call-done), calls=%async_computation.2 | async-start | bytes 2097152 | tf_op jit(solution)/shard_map/all_to_all | solution.py:45
  100.9 30.2 %all-gather.5.cloned.1.call-done = bf16[128,1,8,512]{3,0,1,2:T(8,128)(2,1)} async-done(((bf16[8,1,8,512]{3,0,1,2:T(8,128)(2,1)}), bf16[128,1,8,512]{3,0,1,2:T(8,128)(2,1)}) %all-gather.5.cloned.1.call-update) | async-done | bytes 1048592 | tf_op jit(solution)/shard_map/all_gather | solution.py:40
  131.1 4.2 %all-to-all-start.3 = ((bf16[128,1,8,512]{3,0,1,2:T(8,128)(2,1)}), bf16[128,1,8,512]{3,0,1,2:T(8,128)(2,1)S(1)}, u32[]{:S(2)}, u32[]{:S(2)}) async-start(bf16[128,1,8,512]{3,0,1,2:T(8,128)(2,1)} %all-gather.5.cloned.1.call-done), calls=%async_computation.3 | async-start | bytes 2097152 | tf_op jit(solution)/shard_map/all_to_all | solution.py:46
  135.2 0.2 all-reduce.5.cloned.1.call-start
  135.5 1.1 copy.88
  136.6 26.0 %all-to-all-done.3 = bf16[128,1,8,512]{3,0,1,2:T(8,128)(2,1)S(1)} async-done(((bf16[128,1,8,512]{3,0,1,2:T(8,128)(2,1)}), bf16[128,1,8,512]{3,0,1,2:T(8,128)(2,1)S(1)}, u32[]{:S(2)}, u32[]{:S(2)}) %all-to-all-start.3) | async-done | bytes 1048608 | tf_op jit(solution)/shard_map/all_to_all | solution.py:46
  162.6 1.1 copy.89
  163.7 56.5 %all-reduce.3.cloned.1.call-done = f32[512,1024]{1,0:T(8,128)} async-done(((f32[512,1024]{1,0:T(8,128)}), f32[512,1024]{1,0:T(8,128)}) %all-reduce.3.cloned.1.call-update) | async-done | bytes 2097168 | tf_op jit(solution)/shard_map/psum | solution.py:142
  220.2 2.0 fusion.21
  222.3 0.2 copy-done
  222.4 0.5 multiply_reduce_fusion.1
  223.0 0.5 add_convert_fusion
  223.5 0.7 copy-done.5
  224.2 5.9 %fusion.22 = f32[512,1024]{1,0:T(8,128)} fusion(bf16[1024,512]{1,0:T(8,128)(2,1)} %bitcast.91, bf16[512,1024]{1,0:T(8,128)(2,1)S(1)} %add_convert_fusion, bf16[1024,512]{1,0:T(8,128)(2,1)S(1)} %bitcast.90), kind=kOutput, calls=%fused_computation.44 | convolution fusion | flops 1090781184 | bytes 5242880 | tf_op jit(solution)/shard_map/dot_general | solution.py:160
  230.2 103.9 %all-reduce.5.cloned.1.call-done = f32[512,1024]{1,0:T(8,128)} async-done(((f32[512,1024]{1,0:T(8,128)}), f32[512,1024]{1,0:T(8,128)}) %all-reduce.5.cloned.1.call-update) | async-done | bytes 2097168 | tf_op jit(solution)/shard_map/psum | solution.py:142
  334.0 2.0 fusion.7
  336.1 0.2 copy-done.2
  336.3 0.5 multiply_reduce_fusion
  337.0 0.8 fusion.56
  (54 shorter events, 2.1 us)
Async XLA Ops:
  8.0 89.3 %all-gather.3.cloned.1.call-start = ((), (), s32[]{:S(2)}) async-start(), calls=%async_computation.5 | async-start | bytes 1114112 | tf_op jit(solution)/shard_map/all_gather | solution.py:39
  38.1 29.3 %all-to-all-start.1 = ((bf16[128,1,8,128]{3,0,1,2:T(8,128)(2,1)}), bf16[128,1,8,128]{3,0,1,2:T(8,128)(2,1)S(1)}, u32[]{:S(2)}, u32[]{:S(2)}) async-start(bf16[128,1,8,128]{3,0,1,2:T(8,128)(2,1)} %all_gather.13), calls=%async_computation.1 | async-start | bytes 524288 | tf_op jit(solution)/shard_map/all_to_all | solution.py:44
  43.3 29.9 %copy-start.6 = (f32[8,4096]{1,0:T(8,128)S(1)}, f32[8,4096]{1,0:T(8,128)}, u32[]{:S(2)}) copy-start(f32[8,4096]{1,0:T(8,128)} %param.17) | copy-start | bytes 393220
  44.2 29.8 %copy-start.7 = (s32[512]{0:T(512)S(1)}, s32[512]{0:T(512)}, u32[]{:S(2)}) copy-start(s32[512]{0:T(512)} %param.13) | copy-start | bytes 6148
  67.4 18.4 %all-to-all-start = ((bf16[128,3,8,128]{3,0,1,2:T(8,128)(2,1)}), bf16[128,3,8,128]{3,0,1,2:T(8,128)(2,1)S(1)}, u32[]{:S(2)}, u32[]{:S(2)}) async-start(bf16[128,3,8,128]{3,0,1,2:T(8,128)(2,1)} %copy.76), calls=%async_computation | async-start | bytes 1572864 | tf_op jit(solution)/shard_map/all_to_all | solution.py:43
  73.2 57.9 %all-gather.5.cloned.1.call-start = ((), (), s32[]{:S(2)}) async-start(), calls=%async_computation.6 | async-start | bytes 1114112 | tf_op jit(solution)/shard_map/all_gather | solution.py:40
  73.9 146.3 %all-reduce.3.cloned.1.call-start = ((), (), s32[]{:S(2)}) async-start(), calls=%async_computation.4 | async-start | bytes 4194304 | tf_op jit(solution)/shard_map/psum | solution.py:142
  86.4 1.2 copy-start.1
  88.5 4.9 %copy-start.3 = (bf16[512,128]{1,0:T(8,128)(2,1)}, bf16[512,128]{1,0:T(8,128)(2,1)S(1)}, u32[]{:S(2)}) copy-start(bf16[512,128]{1,0:T(8,128)(2,1)S(1)} %get-tuple-element.157) | copy-start | bytes 393220
  88.5 4.9 %copy-start.4 = (bf16[512,128]{1,0:T(8,128)(2,1)}, bf16[512,128]{1,0:T(8,128)(2,1)S(1)}, u32[]{:S(2)}) copy-start(bf16[512,128]{1,0:T(8,128)(2,1)S(1)} %get-tuple-element.159) | copy-start | bytes 393220
  88.5 4.9 %collective-permute-start = (bf16[512,128]{1,0:T(8,128)(2,1)S(1)}, bf16[512,128]{1,0:T(8,128)(2,1)S(1)}, u32[]{:S(2)}, u32[]{:S(2)}) collective-permute-start(bf16[512,128]{1,0:T(8,128)(2,1)S(1)} %get-tuple-element.159), channel_id=1, source_target_pairs={{0,8},{8,0},{16,24},{24,16},{32,40},{40,32},{48,56},{56,48},{64,72... | collective-permute-start | bytes 393224 | tf_op jit(solution)/shard_map/ppermute | solution.py:11
  90.0 3.3 collective-permute-start.1
  90.6 0.8 copy-start.12
  97.3 33.8 %all-to-all-start.2 = ((bf16[128,1,8,512]{3,0,1,2:T(8,128)(2,1)}), bf16[128,1,8,512]{3,0,1,2:T(8,128)(2,1)S(1)}, u32[]{:S(2)}, u32[]{:S(2)}) async-start(bf16[128,1,8,512]{3,0,1,2:T(8,128)(2,1)} %all-gather.3.cloned.1.call-done), calls=%async_computation.2 | async-start | bytes 2097152 | tf_op jit(solution)/shard_map/all_to_all | solution.py:45
  131.1 31.5 %all-to-all-start.3 = ((bf16[128,1,8,512]{3,0,1,2:T(8,128)(2,1)}), bf16[128,1,8,512]{3,0,1,2:T(8,128)(2,1)S(1)}, u32[]{:S(2)}, u32[]{:S(2)}) async-start(bf16[128,1,8,512]{3,0,1,2:T(8,128)(2,1)} %all-gather.5.cloned.1.call-done), calls=%async_computation.3 | async-start | bytes 2097152 | tf_op jit(solution)/shard_map/all_to_all | solution.py:46
  135.2 198.8 %all-reduce.5.cloned.1.call-start = ((), (), s32[]{:S(2)}) async-start(), calls=%async_computation.7 | async-start | bytes 4194304 | tf_op jit(solution)/shard_map/psum | solution.py:142
  220.2 2.2 copy-start
  222.2 0.7 copy-start.8
  222.3 0.7 copy-start.9
  223.0 1.2 copy-start.5
  334.0 2.2 copy-start.2
  336.3 0.7 copy-start.10
  336.3 0.7 copy-start.11
Sparse Core Ops, SparseCore 0:
  11.1 50.7 all-gather.2
  76.8 54.1 all-gather.4
Sparse Core Ops, SparseCore 1:
  97.4 122.8 all-reduce.2
  230.3 103.7 all-reduce.4
where the time goes:
time: 346 us; the launch traced here: 345 us
  waiting for transfers between devices  225 us (65%)
  blocking collectives  49.9 us (14%)
  starting transfers between devices  20.4 us (6%)
  between operations  17.7 us (5%)
  other arithmetic  11.5 us (3%)
  matrix products  11.2 us (3%)
  local copies, waits for them, and re-layouts  9.31 us (3%)
    psum x2, waiting for transfers between devices, combine(): summed = lax.psum(term_fn(0, tok_rows), 'mp')  160 us
    all_gather x1, waiting for transfers between devices, body(): lax.all_gather(pieces[3], 'group', axis=0, tiled=True)  30.2 us
    all_gather x1, blocking collectives, body(): lax.all_gather(pieces[1], 'group', axis=0, tiled=True)  27.8 us
    all_to_all x1, waiting for transfers between devices, body(): lax.all_to_all(gathered[3], 'mp', split_axis=2, concat_axis=0, tiled=True)  26 us
    all_gather x1, blocking collectives, body(): lax.all_gather(pieces[0], 'group', axis=0, tiled=True)  22.1 us
    all_to_all x1, waiting for transfers between devices, body(): lax.all_to_all(gathered[0], 'mp', split_axis=2, concat_axis=0, tiled=True)  8.33 us
  transfers between devices with their start and end apart: 10, of which 5 were waited for; matrix products, arithmetic and copies ran while one was open for 5% of the time, Pallas kernels for 0%

commit v1 on v0

--- a/solution.py
+++ b/solution.py
@@ -139,7 +139,7 @@
     row_start = lax.axis_index("mp") * share_rows
 
     def combine(term_fn, residual, norm_gain, norm_shift):
-        summed = lax.psum(term_fn(0, tok_rows), "mp")
+        summed = jnp.sum(lax.all_gather(term_fn(0, tok_rows), "mp"), axis=0)
         whole_rows = layer_norm(
             residual.astype(jnp.float32) + summed, norm_gain, norm_shift
         ).astype(jnp.bfloat16)

time: 346 us -> 816 us (2.36)
  waiting for transfers between devices: 225 us -> 684 us
  other arithmetic: 11.5 us -> 24.9 us
    all_gather x0 -> x2, waiting for transfers between devices: none -> 633 us  [combine(): summed = jnp.sum(lax.all_gather(term_fn(0, tok_rows), 'mp'), axis=0)]
    psum x2 -> x0, waiting for transfers between devices: 160 us -> none  [combine(): summed = lax.psum(term_fn(0, tok_rows), 'mp')]
    reduce_sum x0 -> x2, other arithmetic: none -> 16 us  [combine(): summed = jnp.sum(lax.all_gather(term_fn(0, tok_rows), 'mp'), axis=0)]
  transfers between devices with their start and end apart: 10 -> 10, of which waited for: 5 -> 5; matrix products, arithmetic and copies ran while one was open for 5% -> 2% of each run, Pallas kernels for 0% -> 0%
where the time goes in v1:
time: 816 us
  waiting for transfers between devices  684 us (84%)
  blocking collectives  49.9 us (6%)
  other arithmetic  24.9 us (3%)
  starting transfers between devices  20.9 us (3%)
  between operations  16 us (2%)
  matrix products  11.8 us (1%)
  local copies, waits for them, and re-layouts  8.4 us (1%)
    all_gather x2, waiting for transfers between devices, combine(): summed = jnp.sum(lax.all_gather(term_fn(0, tok_rows), 'mp'), axis=0)  633 us
    all_gather x1, blocking collectives, body(): lax.all_gather(pieces[1], 'group', axis=0, tiled=True)  27.7 us
    all_gather x1, waiting for transfers between devices, body(): lax.all_gather(pieces[3], 'group', axis=0, tiled=True)  22.5 us
    all_gather x1, blocking collectives, body(): lax.all_gather(pieces[0], 'group', axis=0, tiled=True)  22.1 us
    all_to_all x1, waiting for transfers between devices, body(): lax.all_to_all(gathered[3], 'mp', split_axis=2, concat_axis=0, tiled=True)  19.4 us
  transfers between devices with their start and end apart: 10, of which 5 were waited for; matrix products, arithmetic and copies ran while one was open for 2% of the time, Pallas kernels for 0%

profile of v1, /device:TPU:1, one launch (start us, length us, event | category | flops | bytes accessed | tf_op | source)
XLA Modules:
  0.0 815.8 jit_solution(12789432771344062430)
XLA Ops:
  7.2 1.5 convert_element_type.73
  8.8 0.8 convert_bitcast_fusion.1
  9.5 27.7 %all_gather.25 = bf16[128,1,8,128]{3,0,1,2:T(8,128)(2,1)} all-gather(bf16[8,1,8,128]{3,0,1,2:T(8,128)(2,1)S(1)} %convert_bitcast_fusion.1), channel_id=1, replica_groups=mesh['group'=16,'mp'=8] {'group'}, dimensions={0}, use_global_device_ids=true | all-gather | bytes 278528 | tf_op jit(solution)/shard_map/all_gather | solution.py:38
  37.3 5.1 all-to-all-start.1
  42.4 0.9 convert_bitcast_fusion
  43.4 22.1 %all_gather.24 = bf16[128,3,8,128]{3,2,1,0:T(8,128)(2,1)S(1)} all-gather(bf16[8,3,8,128]{3,2,1,0:T(8,128)(2,1)S(1)} %bitcast.104), channel_id=1, replica_groups=mesh['group'=16,'mp'=8] {'group'}, dimensions={0}, use_global_device_ids=true | all-gather | bytes 835584 | tf_op jit(solution)/shard_map/all_gather | solution.py:37
  65.5 1.1 copy.76
  66.6 5.7 all-to-all-start
  72.4 0.6 convert_element_type.75
  73.2 0.6 fusion.98
  75.1 0.6 fusion.96
  76.6 8.3 %all-to-all-done = bf16[128,3,8,128]{3,0,1,2:T(8,128)(2,1)S(1)} async-done(((bf16[128,3,8,128]{3,0,1,2:T(8,128)(2,1)}), bf16[128,3,8,128]{3,0,1,2:T(8,128)(2,1)S(1)}, u32[]{:S(2)}, u32[]{:S(2)}) %all-to-all-start) | async-done | bytes 786464 | tf_op jit(solution)/shard_map/all_to_all | solution.py:43
  84.9 0.7 copy.77
  85.6 0.7 reshape.140
  86.4 0.4 copy-done
  86.8 0.7 convolution_convert_fusion
  87.6 1.4 collective-permute-start
  89.5 0.3 fusion.9
  89.8 0.1 convert_reduce_fusion.1
  90.0 0.6 copy-done.10
  90.6 1.5 fusion.10
  92.1 0.2 copy.86
  92.3 0.2 reshape.145
  92.7 2.0 conditional.1
  93.0 0.2 constant_dynamic-slice_fusion
  93.3 0.5 bitcast_reduce_fusion
  93.8 0.4 convert_reduce_fusion
  94.2 0.5 fusion.3
  94.6 1.8 fusion.61
  96.5 3.6 all-to-all-start.2
  100.1 22.5 %all-gather.9.cloned.1.call-done = bf16[128,1,8,512]{3,0,1,2:T(8,128)(2,1)} async-done(((bf16[8,1,8,512]{3,0,1,2:T(8,128)(2,1)}), bf16[128,1,8,512]{3,0,1,2:T(8,128)(2,1)}) %all-gather.9.cloned.1.call-update) | async-done | bytes 1048592 | tf_op jit(solution)/shard_map/all_gather | solution.py:40
  122.6 4.7 all-to-all-start.3
  127.2 0.2 all-gather.13.cloned.1.call-start
  127.5 1.1 copy.88
  128.6 19.4 %all-to-all-done.3 = bf16[128,1,8,512]{3,0,1,2:T(8,128)(2,1)S(1)} async-done(((bf16[128,1,8,512]{3,0,1,2:T(8,128)(2,1)}), bf16[128,1,8,512]{3,0,1,2:T(8,128)(2,1)S(1)}, u32[]{:S(2)}, u32[]{:S(2)}) %all-to-all-start.3) | async-done | bytes 1048608 | tf_op jit(solution)/shard_map/all_to_all | solution.py:46
  147.9 1.1 copy.89
  149.0 307.5 %all-gather.11.cloned.1.call-done = f32[4096,1024]{1,0:T(8,128)} async-done(((f32[512,1024]{1,0:T(8,128)}), f32[4096,1024]{1,0:T(8,128)}) %all-gather.11.cloned.1.call-update) | async-done | bytes 16777232 | tf_op jit(solution)/shard_map/all_gather | solution.py:142
  456.5 8.0 reduce_sum.77
  464.4 0.3 fusion.21
  464.8 0.4 multiply_reduce_fusion.1
  465.2 0.2 copy-done.6
  465.4 1.5 add_convert_fusion
  466.9 6.6 fusion.22
  473.5 325.9 %all-gather.13.cloned.1.call-done = f32[4096,1024]{1,0:T(8,128)} async-done(((f32[512,1024]{1,0:T(8,128)}), f32[4096,1024]{1,0:T(8,128)}) %all-gather.13.cloned.1.call-update) | async-done | bytes 16777232 | tf_op jit(solution)/shard_map/all_gather | solution.py:142
  799.4 8.0 reduce_sum.80
  807.5 0.3 fusion.7
  807.8 0.5 multiply_reduce_fusion
  808.5 0.8 fusion.56
  (52 shorter events, 2.0 us)
Async XLA Ops:
  7.2 89.3 %all-gather.7.cloned.1.call-start = ((), (), s32[]{:S(2)}) async-start(), calls=%async_computation.4 | async-start | bytes 1114112 | tf_op jit(solution)/shard_map/all_gather | solution.py:39
  37.3 29.3 %all-to-all-start.1 = ((bf16[128,1,8,128]{3,0,1,2:T(8,128)(2,1)}), bf16[128,1,8,128]{3,0,1,2:T(8,128)(2,1)S(1)}, u32[]{:S(2)}, u32[]{:S(2)}) async-start(bf16[128,1,8,128]{3,0,1,2:T(8,128)(2,1)} %all_gather.25), calls=%async_computation.1 | async-start | bytes 524288 | tf_op jit(solution)/shard_map/all_to_all | solution.py:44
  42.4 30.0 %copy-start.4 = (f32[8,4096]{1,0:T(8,128)S(1)}, f32[8,4096]{1,0:T(8,128)}, u32[]{:S(2)}) copy-start(f32[8,4096]{1,0:T(8,128)} %param.17) | copy-start | bytes 393220
  43.4 29.8 %copy-start.5 = (s32[512]{0:T(512)S(1)}, s32[512]{0:T(512)}, u32[]{:S(2)}) copy-start(s32[512]{0:T(512)} %param.13) | copy-start | bytes 6148
  66.6 18.3 %all-to-all-start = ((bf16[128,3,8,128]{3,0,1,2:T(8,128)(2,1)}), bf16[128,3,8,128]{3,0,1,2:T(8,128)(2,1)S(1)}, u32[]{:S(2)}, u32[]{:S(2)}) async-start(bf16[128,3,8,128]{3,0,1,2:T(8,128)(2,1)} %copy.76), calls=%async_computation | async-start | bytes 1572864 | tf_op jit(solution)/shard_map/all_to_all | solution.py:43
  72.3 50.2 %all-gather.9.cloned.1.call-start = ((), (), s32[]{:S(2)}) async-start(), calls=%async_computation.5 | async-start | bytes 1114112 | tf_op jit(solution)/shard_map/all_gather | solution.py:40
  73.1 383.4 %all-gather.11.cloned.1.call-start = ((), (), s32[]{:S(2)}) async-start(), calls=%async_computation.6 | async-start | bytes 18874368 | tf_op jit(solution)/shard_map/all_gather | solution.py:142
  85.6 1.2 copy-start
  87.6 4.9 copy-start.2
  87.6 4.9 copy-start.3
  87.6 4.9 collective-permute-start
  89.1 3.4 collective-permute-start.1
  89.8 0.8 copy-start.10
  96.5 26.0 %all-to-all-start.2 = ((bf16[128,1,8,512]{3,0,1,2:T(8,128)(2,1)}), bf16[128,1,8,512]{3,0,1,2:T(8,128)(2,1)S(1)}, u32[]{:S(2)}, u32[]{:S(2)}) async-start(bf16[128,1,8,512]{3,0,1,2:T(8,128)(2,1)} %all-gather.7.cloned.1.call-done), calls=%async_computation.2 | async-start | bytes 2097152 | tf_op jit(solution)/shard_map/all_to_all | solution.py:45
  122.6 25.4 %all-to-all-start.3 = ((bf16[128,1,8,512]{3,0,1,2:T(8,128)(2,1)}), bf16[128,1,8,512]{3,0,1,2:T(8,128)(2,1)S(1)}, u32[]{:S(2)}, u32[]{:S(2)}) async-start(bf16[128,1,8,512]{3,0,1,2:T(8,128)(2,1)} %all-gather.9.cloned.1.call-done), calls=%async_computation.3 | async-start | bytes 2097152 | tf_op jit(solution)/shard_map/all_to_all | solution.py:46
  127.2 672.2 %all-gather.13.cloned.1.call-start = ((), (), s32[]{:S(2)}) async-start(), calls=%async_computation.7 | async-start | bytes 18874368 | tf_op jit(solution)/shard_map/all_gather | solution.py:142
  464.7 0.7 copy-start.6
  464.7 0.7 copy-start.7
  799.4 8.0 copy-start.1
  807.8 0.7 copy-start.8
  807.8 0.7 copy-start.9
Sparse Core Ops, SparseCore 0:
  10.3 50.6 all-gather.6
  76.0 46.5 all-gather.8
  124.2 332.2 all-gather.10
  473.6 325.7 all-gather.12
